TPU v7x, 512 devices: a whole 4x4x16 slice. The times are simulated.
512 devices in a mesh: ev: 8 (over y_hi, x), sp: 64 (over z, y_lo, core).
Axes of the slice: x: 4, y: 4 (y_hi: 2, y_lo: 2; y = y_hi * 2 + y_lo), z: 16, core: 2. Of those that a mesh axis runs over, the one named last changes fastest.
Arguments:
- partial_kernels: float32 [8, 32, 512, 128], P('ev', None, 'sp'), may hold values from -6 to 6
- block_ids: int32 [8, 512], P('ev', 'sp'), may hold values from 0 to 255, as said below
- radial_smoother: float32 [128, 128], replicated, may hold values from -0.5 to 2
- shell_level: int32 [128], P('sp'), may hold values from 1 to 4
- lateral_scale: float32 [512, 1024], replicated, may hold values from 0.5 to 1
Outputs:
- smoothed_kernel: float32 [128, 512, 1024], P('sp', None, 'ev')
Inputs may be any that keep to these rules, and one draw needn't show every extreme that they name: `block_ids`: each index of ev and sp holds 8 distinct ids; an id's owner is id // 32; one holder gives at most 2 ids to one owner, and in every stripe some owner receives 2 ids from every group.
All inputs are finite; a program needn't handle non-finite values.
Results may differ from a plain program's by a relative error of at most 0.000073.
Values sent between devices are 32-bit elements; how exact they have to be, the bound alone decides.
No kernel may reach another device: no remote copies, remote signals or barrier semaphores. Data moves between devices by JAX's collectives and lax.ppermute only.
A program may use at most 64 MiB of HBM per device.

v0:
```python
import jax
import jax.numpy as jnp
from jax import lax
from jax.sharding import PartitionSpec as P

NR = 128
BPT = 8
CAP = 2
PASSES = 4
NSEG = 4
diffusion_rate = 0.0615


def padded_2(cells, sides, width):
    for axis, dim in sides:
        count = lax.axis_size(axis)
        ends = count - 1
        head = lax.slice_in_dim(cells, 0, width, axis=dim)
        tail = lax.slice_in_dim(cells, cells.shape[dim] - width, cells.shape[dim], axis=dim)
        cells = jnp.concatenate(
            [
                lax.ppermute(tail, axis, [(i, (i + 1) % count) for i in range(ends)]),
                cells,
                lax.ppermute(head, axis, [((i + 1) % count, i) for i in range(ends)]),
            ],
            axis=dim,
        )
    return cells


def per_device(partial_kernels, block_ids, radial_smoother, shell_level, lateral_scale):
    groups = lax.axis_size("ev")
    per_owner = BPT * NSEG
    blocks = partial_kernels[0]
    block_list = block_ids[0]
    owners = block_list // per_owner
    within = block_list % per_owner
    listed = block_list.shape[0]
    same_owner = owners[:, None] == owners[None, :]
    earlier = jnp.arange(listed)[None, :] < jnp.arange(listed)[:, None]
    ranking = jnp.sum(same_owner & earlier, axis=1)
    slot_of = owners * CAP + ranking
    placing = (slot_of[None, :] == jnp.arange(groups * CAP, dtype=jnp.int32)[:, None]).astype(
        jnp.float32
    )
    packed = jnp.einsum("rjc,sj->rsc", blocks, placing, precision=lax.Precision.HIGHEST)
    label_out = (
        jnp.dot(placing, within.astype(jnp.float32) + 1.0, precision=lax.Precision.HIGHEST) - 1.0
    )
    label_out = label_out.reshape(1, groups * CAP, 1)
    arrived, labels = (
        lax.all_to_all(packed, "ev", split_axis=1, concat_axis=1, tiled=True),
        lax.all_to_all(label_out, "ev", split_axis=1, concat_axis=1, tiled=True),
    )
    picker = (labels.reshape(1, -1) == jnp.arange(per_owner, dtype=jnp.float32)[:, None]).astype(
        jnp.float32
    )
    column_tile = jnp.einsum("rsc,ls->lrc", arrived, picker, precision=lax.Precision.HIGHEST)
    tile_width = column_tile.shape[2]
    columns = column_tile.reshape(BPT, NR, tile_width)
    smoothed = jnp.einsum("rq,kqc->rkc", radial_smoother, columns, precision=lax.Precision.HIGHEST)
    shells = lax.all_to_all(smoothed, "sp", split_axis=0, concat_axis=1, tiled=True)
    ev_index = lax.axis_index("ev")
    levels = shell_level.astype(jnp.float32)[:, None, None]
    scale_here = lax.dynamic_slice_in_dim(lateral_scale, ev_index * tile_width, tile_width, 1)
    coefficient = diffusion_rate * levels * scale_here[None]
    kernel_field = shells
    for repeat in range(PASSES):
        padded = padded_2(kernel_field, (("ev", 2),), 1)
        padded = jnp.pad(padded, ((0, 0), (1, 1), (0, 0)))
        beside = (
            padded[:, 2:, 1:-1] + padded[:, :-2, 1:-1] + padded[:, 1:-1, 2:] + padded[:, 1:-1, :-2]
        )
        kernel_field = kernel_field + coefficient * (beside - 4.0 * kernel_field)
    return kernel_field


def solution(mesh):
    placed = (P("ev", None, "sp", None), P("ev", "sp"), P(), P("sp"), P())
    return jax.shard_map(
        per_device, mesh=mesh, in_specs=placed, out_specs=P("sp", None, "ev"), check_vma=False
    )
```

profile of v0, /device:TPU:88, one launch (start us, length us, event | category | flops | bytes accessed | tf_op | source)
XLA Modules:
  0.0 168.2 jit_solution(15304359649547561368)
XLA Ops:
  0.0 0.8 fusion.47
  2.3 0.8 fusion.1
  3.9 7.3 %all-to-all-start = ((f32[1,16,1]{2,0,1:T(1,128)}), f32[1,16,1]{2,0,1:T(1,128)S(1)}, u32[]{:S(2)}, u32[]{:S(2)}) async-start(f32[1,16,1]{2,0,1:T(1,128)} %copy.28), calls=%async_computation | async-start | bytes 16384 | tf_op jit(solution)/shard_map/all_to_all | solution.py:53
  11.1 1.3 convolution_bitcast_fusion.1
  12.4 0.8 copy.29
  13.2 2.7 %all-to-all-done = f32[1,16,1]{2,0,1:T(1,128)S(1)} async-done(((f32[1,16,1]{2,0,1:T(1,128)}), f32[1,16,1]{2,0,1:T(1,128)S(1)}, u32[]{:S(2)}, u32[]{:S(2)}) %all-to-all-start) | async-done | bytes 96 | tf_op jit(solution)/shard_map/all_to_all | solution.py:53
  15.8 6.3 %all-to-all-start.1 = ((f32[32,16,128]{2,0,1:T(8,128)}), f32[32,16,128]{2,0,1:T(8,128)S(1)}, u32[]{:S(2)}, u32[]{:S(2)}) async-start(f32[32,16,128]{2,0,1:T(8,128)} %copy.29), calls=%async_computation.1 | async-start | bytes 524288 | tf_op jit(solution)/shard_map/all_to_all | solution.py:52
  22.4 5.6 %all-to-all-done.1 = f32[32,16,128]{2,0,1:T(8,128)S(1)} async-done(((f32[32,16,128]{2,0,1:T(8,128)}), f32[32,16,128]{2,0,1:T(8,128)S(1)}, u32[]{:S(2)}, u32[]{:S(2)}) %all-to-all-start.1) | async-done | bytes 262176 | tf_op jit(solution)/shard_map/all_to_all | solution.py:52
  28.9 1.0 convolution_bitcast_fusion
  29.9 1.0 copy.33
  30.9 16.2 %all-to-all-start.2 = ((f32[128,8,128]{2,1,0:T(8,128)}), f32[128,8,128]{2,1,0:T(8,128)S(1)}, u32[]{:S(2)}, u32[]{:S(2)}) async-start(f32[128,8,128]{2,1,0:T(8,128)} %copy.33), calls=%async_computation.2 | async-start | bytes 1048576 | tf_op jit(solution)/shard_map/all_to_all | solution.py:62
  47.1 29.4 %all-to-all-done.2 = f32[128,8,128]{2,1,0:T(8,128)S(1)} async-done(((f32[128,8,128]{2,1,0:T(8,128)}), f32[128,8,128]{2,1,0:T(8,128)S(1)}, u32[]{:S(2)}, u32[]{:S(2)}) %all-to-all-start.2) | async-done | bytes 524320 | tf_op jit(solution)/shard_map/all_to_all | solution.py:62
  76.7 5.4 %collective-permute-start.1 = (f32[2,512,1]{2,1,0:T(8,128)S(1)}, f32[2,512,1]{2,1,0:T(8,128)S(1)}, u32[]{:S(2)}, u32[]{:S(2)}) collective-permute-start(f32[2,512,1]{2,1,0:T(8,128)S(1)} %get-tuple-element.11), channel_id=1, source_target_pairs={{64,0},{128,64},{192,128},{256,192},{320,256},{384,320},{448,384},... | collective-permute-start | bytes 12296 | tf_op jit(solution)/shard_map/ppermute | solution.py:24
  82.1 1.9 %collective-permute-start = (f32[2,512,1]{2,1,0:T(8,128)S(1)}, f32[2,512,1]{2,1,0:T(8,128)S(1)}, u32[]{:S(2)}, u32[]{:S(2)}) collective-permute-start(f32[2,512,1]{2,1,0:T(8,128)S(1)} %get-tuple-element.12), channel_id=1, source_target_pairs={{0,64},{64,128},{128,192},{192,256},{256,320},{320,384},{384,448},... | collective-permute-start | bytes 12296 | tf_op jit(solution)/shard_map/ppermute | solution.py:22
  84.1 10.0 %collective-permute-done.1 = f32[2,512,1]{2,1,0:T(8,128)S(1)} collective-permute-done((f32[2,512,1]{2,1,0:T(8,128)S(1)}, f32[2,512,1]{2,1,0:T(8,128)S(1)}, u32[]{:S(2)}, u32[]{:S(2)}) %collective-permute-start.1) | collective-permute-done | bytes 4128 | tf_op jit(solution)/shard_map/ppermute | solution.py:24
  94.1 7.7 %collective-permute-done = f32[2,512,1]{2,1,0:T(8,128)S(1)} collective-permute-done((f32[2,512,1]{2,1,0:T(8,128)S(1)}, f32[2,512,1]{2,1,0:T(8,128)S(1)}, u32[]{:S(2)}, u32[]{:S(2)}) %collective-permute-start) | collective-permute-done | bytes 4128 | tf_op jit(solution)/shard_map/ppermute | solution.py:22
  102.4 0.8 fusion.3
  103.3 1.9 %collective-permute-start.3 = (f32[2,512,1]{2,1,0:T(8,128)S(1)}, f32[2,512,1]{2,1,0:T(8,128)S(1)}, u32[]{:S(2)}, u32[]{:S(2)}) collective-permute-start(f32[2,512,1]{2,1,0:T(8,128)S(1)} %get-tuple-element.9), channel_id=1, source_target_pairs={{64,0},{128,64},{192,128},{256,192},{320,256},{384,320},{448,384},... | collective-permute-start | bytes 12296 | tf_op jit(solution)/shard_map/ppermute | solution.py:24
  105.3 3.9 %collective-permute-start.2 = (f32[2,512,1]{2,1,0:T(8,128)S(1)}, f32[2,512,1]{2,1,0:T(8,128)S(1)}, u32[]{:S(2)}, u32[]{:S(2)}) collective-permute-start(f32[2,512,1]{2,1,0:T(8,128)S(1)} %get-tuple-element.10), channel_id=1, source_target_pairs={{0,64},{64,128},{128,192},{192,256},{256,320},{320,384},{384,448},... | collective-permute-start | bytes 12296 | tf_op jit(solution)/shard_map/ppermute | solution.py:22
  109.2 9.4 %collective-permute-done.3 = f32[2,512,1]{2,1,0:T(8,128)S(1)} collective-permute-done((f32[2,512,1]{2,1,0:T(8,128)S(1)}, f32[2,512,1]{2,1,0:T(8,128)S(1)}, u32[]{:S(2)}, u32[]{:S(2)}) %collective-permute-start.3) | collective-permute-done | bytes 4128 | tf_op jit(solution)/shard_map/ppermute | solution.py:24
  118.6 5.5 %collective-permute-done.2 = f32[2,512,1]{2,1,0:T(8,128)S(1)} collective-permute-done((f32[2,512,1]{2,1,0:T(8,128)S(1)}, f32[2,512,1]{2,1,0:T(8,128)S(1)}, u32[]{:S(2)}, u32[]{:S(2)}) %collective-permute-start.2) | collective-permute-done | bytes 4128 | tf_op jit(solution)/shard_map/ppermute | solution.py:22
  124.6 0.8 fusion.4
  125.6 1.9 %collective-permute-start.5 = (f32[2,512,1]{2,1,0:T(8,128)S(1)}, f32[2,512,1]{2,1,0:T(8,128)S(1)}, u32[]{:S(2)}, u32[]{:S(2)}) collective-permute-start(f32[2,512,1]{2,1,0:T(8,128)S(1)} %get-tuple-element.7), channel_id=1, source_target_pairs={{64,0},{128,64},{192,128},{256,192},{320,256},{384,320},{448,384},... | collective-permute-start | bytes 12296 | tf_op jit(solution)/shard_map/ppermute | solution.py:24
  127.6 3.9 %collective-permute-start.4 = (f32[2,512,1]{2,1,0:T(8,128)S(1)}, f32[2,512,1]{2,1,0:T(8,128)S(1)}, u32[]{:S(2)}, u32[]{:S(2)}) collective-permute-start(f32[2,512,1]{2,1,0:T(8,128)S(1)} %get-tuple-element.8), channel_id=1, source_target_pairs={{0,64},{64,128},{128,192},{192,256},{256,320},{320,384},{384,448},... | collective-permute-start | bytes 12296 | tf_op jit(solution)/shard_map/ppermute | solution.py:22
  131.5 8.6 %collective-permute-done.5 = f32[2,512,1]{2,1,0:T(8,128)S(1)} collective-permute-done((f32[2,512,1]{2,1,0:T(8,128)S(1)}, f32[2,512,1]{2,1,0:T(8,128)S(1)}, u32[]{:S(2)}, u32[]{:S(2)}) %collective-permute-start.5) | collective-permute-done | bytes 4128 | tf_op jit(solution)/shard_map/ppermute | solution.py:24
  140.0 5.5 %collective-permute-done.4 = f32[2,512,1]{2,1,0:T(8,128)S(1)} collective-permute-done((f32[2,512,1]{2,1,0:T(8,128)S(1)}, f32[2,512,1]{2,1,0:T(8,128)S(1)}, u32[]{:S(2)}, u32[]{:S(2)}) %collective-permute-start.4) | collective-permute-done | bytes 4128 | tf_op jit(solution)/shard_map/ppermute | solution.py:22
  146.1 0.8 fusion.5
  147.1 1.9 %collective-permute-start.7 = (f32[2,512,1]{2,1,0:T(8,128)S(1)}, f32[2,512,1]{2,1,0:T(8,128)S(1)}, u32[]{:S(2)}, u32[]{:S(2)}) collective-permute-start(f32[2,512,1]{2,1,0:T(8,128)S(1)} %get-tuple-element.5), channel_id=1, source_target_pairs={{64,0},{128,64},{192,128},{256,192},{320,256},{384,320},{448,384},... | collective-permute-start | bytes 12296 | tf_op jit(solution)/shard_map/ppermute | solution.py:24
  149.0 3.9 %collective-permute-start.6 = (f32[2,512,1]{2,1,0:T(8,128)S(1)}, f32[2,512,1]{2,1,0:T(8,128)S(1)}, u32[]{:S(2)}, u32[]{:S(2)}) collective-permute-start(f32[2,512,1]{2,1,0:T(8,128)S(1)} %get-tuple-element.6), channel_id=1, source_target_pairs={{0,64},{64,128},{128,192},{192,256},{256,320},{320,384},{384,448},... | collective-permute-start | bytes 12296 | tf_op jit(solution)/shard_map/ppermute | solution.py:22
  152.9 7.7 %collective-permute-done.7 = f32[2,512,1]{2,1,0:T(8,128)S(1)} collective-permute-done((f32[2,512,1]{2,1,0:T(8,128)S(1)}, f32[2,512,1]{2,1,0:T(8,128)S(1)}, u32[]{:S(2)}, u32[]{:S(2)}) %collective-permute-start.7) | collective-permute-done | bytes 4128 | tf_op jit(solution)/shard_map/ppermute | solution.py:24
  160.6 5.5 %collective-permute-done.6 = f32[2,512,1]{2,1,0:T(8,128)S(1)} collective-permute-done((f32[2,512,1]{2,1,0:T(8,128)S(1)}, f32[2,512,1]{2,1,0:T(8,128)S(1)}, u32[]{:S(2)}, u32[]{:S(2)}) %collective-permute-start.6) | collective-permute-done | bytes 4128 | tf_op jit(solution)/shard_map/ppermute | solution.py:22
  166.6 1.5 fusion.6
  (24 shorter events, 6.1 us)
Async XLA Ops:
  0.0 84.1 %copy-start = (f32[512,1024]{1,0:T(8,128)S(1)}, f32[512,1024]{1,0:T(8,128)}, u32[]{:S(2)}) copy-start(f32[512,1024]{1,0:T(8,128)} %param.9) | copy-start | bytes 6291460
  3.9 12.0 %all-to-all-start = ((f32[1,16,1]{2,0,1:T(1,128)}), f32[1,16,1]{2,0,1:T(1,128)S(1)}, u32[]{:S(2)}, u32[]{:S(2)}) async-start(f32[1,16,1]{2,0,1:T(1,128)} %copy.28), calls=%async_computation | async-start | bytes 16384 | tf_op jit(solution)/shard_map/all_to_all | solution.py:53
  13.2 15.7 %copy-start.1 = (f32[128,128]{1,0:T(8,128)S(1)}, f32[128,128]{1,0:T(8,128)}, u32[]{:S(2)}) copy-start(f32[128,128]{1,0:T(8,128)} %param.7) | copy-start | bytes 196612
  15.8 12.1 %all-to-all-start.1 = ((f32[32,16,128]{2,0,1:T(8,128)}), f32[32,16,128]{2,0,1:T(8,128)S(1)}, u32[]{:S(2)}, u32[]{:S(2)}) async-start(f32[32,16,128]{2,0,1:T(8,128)} %copy.29), calls=%async_computation.1 | async-start | bytes 524288 | tf_op jit(solution)/shard_map/all_to_all | solution.py:52
  29.9 17.2 %copy-start.2 = (s32[2]{0:T(128)S(1)}, s32[2]{0:T(128)}, u32[]{:S(2)}) copy-start(s32[2]{0:T(128)} %param.8) | copy-start | bytes 28
  30.9 45.6 %all-to-all-start.2 = ((f32[128,8,128]{2,1,0:T(8,128)}), f32[128,8,128]{2,1,0:T(8,128)S(1)}, u32[]{:S(2)}, u32[]{:S(2)}) async-start(f32[128,8,128]{2,1,0:T(8,128)} %copy.33), calls=%async_computation.2 | async-start | bytes 1048576 | tf_op jit(solution)/shard_map/all_to_all | solution.py:62
  76.7 17.4 %collective-permute-start.1 = (f32[2,512,1]{2,1,0:T(8,128)S(1)}, f32[2,512,1]{2,1,0:T(8,128)S(1)}, u32[]{:S(2)}, u32[]{:S(2)}) collective-permute-start(f32[2,512,1]{2,1,0:T(8,128)S(1)} %get-tuple-element.11), channel_id=1, source_target_pairs={{64,0},{128,64},{192,128},{256,192},{320,256},{384,320},{448,384},... | collective-permute-start | bytes 12296 | tf_op jit(solution)/shard_map/ppermute | solution.py:24
  82.1 19.7 %collective-permute-start = (f32[2,512,1]{2,1,0:T(8,128)S(1)}, f32[2,512,1]{2,1,0:T(8,128)S(1)}, u32[]{:S(2)}, u32[]{:S(2)}) collective-permute-start(f32[2,512,1]{2,1,0:T(8,128)S(1)} %get-tuple-element.12), channel_id=1, source_target_pairs={{0,64},{64,128},{128,192},{192,256},{256,320},{320,384},{384,448},... | collective-permute-start | bytes 12296 | tf_op jit(solution)/shard_map/ppermute | solution.py:22
  103.3 15.3 %collective-permute-start.3 = (f32[2,512,1]{2,1,0:T(8,128)S(1)}, f32[2,512,1]{2,1,0:T(8,128)S(1)}, u32[]{:S(2)}, u32[]{:S(2)}) collective-permute-start(f32[2,512,1]{2,1,0:T(8,128)S(1)} %get-tuple-element.9), channel_id=1, source_target_pairs={{64,0},{128,64},{192,128},{256,192},{320,256},{384,320},{448,384},... | collective-permute-start | bytes 12296 | tf_op jit(solution)/shard_map/ppermute | solution.py:24
  105.3 18.9 %collective-permute-start.2 = (f32[2,512,1]{2,1,0:T(8,128)S(1)}, f32[2,512,1]{2,1,0:T(8,128)S(1)}, u32[]{:S(2)}, u32[]{:S(2)}) collective-permute-start(f32[2,512,1]{2,1,0:T(8,128)S(1)} %get-tuple-element.10), channel_id=1, source_target_pairs={{0,64},{64,128},{128,192},{192,256},{256,320},{320,384},{384,448},... | collective-permute-start | bytes 12296 | tf_op jit(solution)/shard_map/ppermute | solution.py:22
  125.6 14.4 %collective-permute-start.5 = (f32[2,512,1]{2,1,0:T(8,128)S(1)}, f32[2,512,1]{2,1,0:T(8,128)S(1)}, u32[]{:S(2)}, u32[]{:S(2)}) collective-permute-start(f32[2,512,1]{2,1,0:T(8,128)S(1)} %get-tuple-element.7), channel_id=1, source_target_pairs={{64,0},{128,64},{192,128},{256,192},{320,256},{384,320},{448,384},... | collective-permute-start | bytes 12296 | tf_op jit(solution)/shard_map/ppermute | solution.py:24
  127.6 18.0 %collective-permute-start.4 = (f32[2,512,1]{2,1,0:T(8,128)S(1)}, f32[2,512,1]{2,1,0:T(8,128)S(1)}, u32[]{:S(2)}, u32[]{:S(2)}) collective-permute-start(f32[2,512,1]{2,1,0:T(8,128)S(1)} %get-tuple-element.8), channel_id=1, source_target_pairs={{0,64},{64,128},{128,192},{192,256},{256,320},{320,384},{384,448},... | collective-permute-start | bytes 12296 | tf_op jit(solution)/shard_map/ppermute | solution.py:22
  147.1 13.6 %collective-permute-start.7 = (f32[2,512,1]{2,1,0:T(8,128)S(1)}, f32[2,512,1]{2,1,0:T(8,128)S(1)}, u32[]{:S(2)}, u32[]{:S(2)}) collective-permute-start(f32[2,512,1]{2,1,0:T(8,128)S(1)} %get-tuple-element.5), channel_id=1, source_target_pairs={{64,0},{128,64},{192,128},{256,192},{320,256},{384,320},{448,384},... | collective-permute-start | bytes 12296 | tf_op jit(solution)/shard_map/ppermute | solution.py:24
  149.0 17.2 %collective-permute-start.6 = (f32[2,512,1]{2,1,0:T(8,128)S(1)}, f32[2,512,1]{2,1,0:T(8,128)S(1)}, u32[]{:S(2)}, u32[]{:S(2)}) collective-permute-start(f32[2,512,1]{2,1,0:T(8,128)S(1)} %get-tuple-element.6), channel_id=1, source_target_pairs={{0,64},{64,128},{128,192},{192,256},{256,320},{320,384},{384,448},... | collective-permute-start | bytes 12296 | tf_op jit(solution)/shard_map/ppermute | solution.py:22
where the time goes:
time: 169 us; the launch traced here: 168 us
  waiting for transfers between devices  97.7 us (58%)
  starting transfers between devices  54.6 us (32%)
  other arithmetic  8.32 us (5%)
  local copies, waits for them, and re-layouts  3.67 us (2%)
  matrix products  3.66 us (2%)
    ppermute x4, waiting for transfers between devices, padded_2(): lax.ppermute(head, axis, [((i + 1) % count, i) for i in range(ends)])  35.7 us
    all_to_all x1, waiting for transfers between devices, per_device(): lax.all_to_all(smoothed, 'sp', split_axis=0, concat_axis=1, tiled=True)  29.4 us
    ppermute x4, waiting for transfers between devices, padded_2(): lax.ppermute(tail, axis, [(i, (i + 1) % count) for i in range(ends)])  24.4 us
    all_to_all x1, starting transfers between devices, per_device(): lax.all_to_all(smoothed, 'sp', split_axis=0, concat_axis=1, tiled=True)  16.2 us
    ppermute x4, starting transfers between devices, padded_2(): lax.ppermute(tail, axis, [(i, (i + 1) % count) for i in range(ends)])  13.7 us
    ppermute x4, starting transfers between devices, padded_2(): lax.ppermute(head, axis, [((i + 1) % count, i) for i in range(ends)])  11.2 us
    all_to_all x1, starting transfers between devices, per_device(): lax.all_to_all(label_out, 'ev', split_axis=1, concat_axis=1, tiled=True)  7.26 us
    all_to_all x1, starting transfers between devices, per_device(): lax.all_to_all(packed, 'ev', split_axis=1, concat_axis=1, tiled=True)  6.3 us
  transfers between devices with their start and end apart: 11, of which 11 were waited for; matrix products, arithmetic and copies ran while one was open for 1% of the time, Pallas kernels for 0%

commit v1 on v0

--- a/solution.py
+++ b/solution.py
@@ -9,6 +9,12 @@
 PASSES = 4
 NSEG = 4
 diffusion_rate = 0.0615
+
+
+def swap_blocks(block, axis, split, join):
+    shards = jnp.split(block, lax.axis_size(axis), axis=split)
+    incoming = lax.all_to_all(jnp.stack(shards), axis, 0, 0)
+    return jnp.concatenate(incoming, axis=join)
 
 
 def padded_2(cells, sides, width):
@@ -50,7 +56,7 @@
     label_out = label_out.reshape(1, groups * CAP, 1)
     arrived, labels = (
         lax.all_to_all(packed, "ev", split_axis=1, concat_axis=1, tiled=True),
-        lax.all_to_all(label_out, "ev", split_axis=1, concat_axis=1, tiled=True),
+        swap_blocks(label_out, "ev", 1, 1),
     )
     picker = (labels.reshape(1, -1) == jnp.arange(per_owner, dtype=jnp.float32)[:, None]).astype(
         jnp.float32

time: 169 us -> 173 us (1.024)
  local copies, waits for them, and re-layouts: 3.67 us -> 8.48 us
    unnamed x6 -> x13, local copies, waits for them, and re-layouts: 0.01 us -> 4.27 us
  transfers between devices with their start and end apart: 11 -> 11, of which waited for: 11 -> 11; matrix products, arithmetic and copies ran while one was open for 1% -> 2% of each run, Pallas kernels for 0% -> 0%
where the time goes in v1:
time: 173 us; the launch traced here: 172 us
  waiting for transfers between devices  96.6 us (56%)
  starting transfers between devices  54.6 us (32%)
  other arithmetic  8.75 us (5%)
  local copies, waits for them, and re-layouts  8.48 us (5%)
  matrix products  3.66 us (2%)
    ppermute x4, waiting for transfers between devices, padded_2(): lax.ppermute(head, axis, [((i + 1) % count, i) for i in range(ends)])  35.7 us
    all_to_all x1, waiting for transfers between devices, per_device(): lax.all_to_all(smoothed, 'sp', split_axis=0, concat_axis=1, tiled=True)  29.4 us
    ppermute x4, waiting for transfers between devices, padded_2(): lax.ppermute(tail, axis, [(i, (i + 1) % count) for i in range(ends)])  24.4 us
    all_to_all x1, starting transfers between devices, per_device(): lax.all_to_all(smoothed, 'sp', split_axis=0, concat_axis=1, tiled=True)  16.2 us
    ppermute x4, starting transfers between devices, padded_2(): lax.ppermute(tail, axis, [(i, (i + 1) % count) for i in range(ends)])  13.7 us
    ppermute x4, starting transfers between devices, padded_2(): lax.ppermute(head, axis, [((i + 1) % count, i) for i in range(ends)])  11.2 us
    all_to_all x1, starting transfers between devices, swap_blocks(): incoming = lax.all_to_all(jnp.stack(shards), axis, 0, 0)  7.26 us
    all_to_all x1, starting transfers between devices, per_device(): lax.all_to_all(packed, 'ev', split_axis=1, concat_axis=1, tiled=True)  6.31 us
  transfers between devices with their start and end apart: 11, of which 11 were waited for; matrix products, arithmetic and copies ran while one was open for 2% of the time, Pallas kernels for 0%

profile of v1, /device:TPU:88, one launch (start us, length us, event | category | flops | bytes accessed | tf_op | source)
XLA Modules:
  0.0 172.3 jit_solution(16212414447941072230)
XLA Ops:
  0.0 0.8 fusion.47
  2.3 0.8 fusion.1
  8.0 7.3 %all-to-all-start = ((f32[8,1,2,1]{2,3,1,0:T(1,128)}), f32[8,1,2,1]{2,3,1,0:T(1,128)S(1)}, u32[]{:S(2)}, u32[]{:S(2)}) async-start(f32[8,1,2,1]{2,3,1,0:T(1,128)} %constant_dynamic-update-slice_fusion), calls=%async_computation | async-start | bytes 8192 | tf_op jit(solution)/shard_map/all_to_all | solution.py:16
  15.3 1.3 convolution_bitcast_fusion.1
  16.6 0.8 copy.44
  17.4 2.6 %all-to-all-done = f32[8,1,2,1]{2,3,1,0:T(1,128)S(1)} async-done(((f32[8,1,2,1]{2,3,1,0:T(1,128)}), f32[8,1,2,1]{2,3,1,0:T(1,128)S(1)}, u32[]{:S(2)}, u32[]{:S(2)}) %all-to-all-start) | async-done | bytes 96 | tf_op jit(solution)/shard_map/all_to_all | solution.py:16
  20.0 6.3 %all-to-all-start.1 = ((f32[32,16,128]{2,0,1:T(8,128)}), f32[32,16,128]{2,0,1:T(8,128)S(1)}, u32[]{:S(2)}, u32[]{:S(2)}) async-start(f32[32,16,128]{2,0,1:T(8,128)} %copy.44), calls=%async_computation.1 | async-start | bytes 524288 | tf_op jit(solution)/shard_map/all_to_all | solution.py:58
  27.6 4.5 %all-to-all-done.1 = f32[32,16,128]{2,0,1:T(8,128)S(1)} async-done(((f32[32,16,128]{2,0,1:T(8,128)}), f32[32,16,128]{2,0,1:T(8,128)S(1)}, u32[]{:S(2)}, u32[]{:S(2)}) %all-to-all-start.1) | async-done | bytes 262176 | tf_op jit(solution)/shard_map/all_to_all | solution.py:58
  33.0 1.0 convolution_bitcast_fusion
  34.0 1.0 copy.48
  35.0 16.2 %all-to-all-start.2 = ((f32[128,8,128]{2,1,0:T(8,128)}), f32[128,8,128]{2,1,0:T(8,128)S(1)}, u32[]{:S(2)}, u32[]{:S(2)}) async-start(f32[128,8,128]{2,1,0:T(8,128)} %copy.48), calls=%async_computation.2 | async-start | bytes 1048576 | tf_op jit(solution)/shard_map/all_to_all | solution.py:68
  51.3 29.4 %all-to-all-done.2 = f32[128,8,128]{2,1,0:T(8,128)S(1)} async-done(((f32[128,8,128]{2,1,0:T(8,128)}), f32[128,8,128]{2,1,0:T(8,128)S(1)}, u32[]{:S(2)}, u32[]{:S(2)}) %all-to-all-start.2) | async-done | bytes 524320 | tf_op jit(solution)/shard_map/all_to_all | solution.py:68
  80.9 5.4 %collective-permute-start.1 = (f32[2,512,1]{2,1,0:T(8,128)S(1)}, f32[2,512,1]{2,1,0:T(8,128)S(1)}, u32[]{:S(2)}, u32[]{:S(2)}) collective-permute-start(f32[2,512,1]{2,1,0:T(8,128)S(1)} %get-tuple-element.11), channel_id=1, source_target_pairs={{64,0},{128,64},{192,128},{256,192},{320,256},{384,320},{448,384},... | collective-permute-start | bytes 12296 | tf_op jit(solution)/shard_map/ppermute | solution.py:30
  86.3 1.9 %collective-permute-start = (f32[2,512,1]{2,1,0:T(8,128)S(1)}, f32[2,512,1]{2,1,0:T(8,128)S(1)}, u32[]{:S(2)}, u32[]{:S(2)}) collective-permute-start(f32[2,512,1]{2,1,0:T(8,128)S(1)} %get-tuple-element.12), channel_id=1, source_target_pairs={{0,64},{64,128},{128,192},{192,256},{256,320},{320,384},{384,448},... | collective-permute-start | bytes 12296 | tf_op jit(solution)/shard_map/ppermute | solution.py:28
  88.3 10.0 %collective-permute-done.1 = f32[2,512,1]{2,1,0:T(8,128)S(1)} collective-permute-done((f32[2,512,1]{2,1,0:T(8,128)S(1)}, f32[2,512,1]{2,1,0:T(8,128)S(1)}, u32[]{:S(2)}, u32[]{:S(2)}) %collective-permute-start.1) | collective-permute-done | bytes 4128 | tf_op jit(solution)/shard_map/ppermute | solution.py:30
  98.3 7.7 %collective-permute-done = f32[2,512,1]{2,1,0:T(8,128)S(1)} collective-permute-done((f32[2,512,1]{2,1,0:T(8,128)S(1)}, f32[2,512,1]{2,1,0:T(8,128)S(1)}, u32[]{:S(2)}, u32[]{:S(2)}) %collective-permute-start) | collective-permute-done | bytes 4128 | tf_op jit(solution)/shard_map/ppermute | solution.py:28
  106.5 0.8 fusion.3
  107.5 1.9 %collective-permute-start.3 = (f32[2,512,1]{2,1,0:T(8,128)S(1)}, f32[2,512,1]{2,1,0:T(8,128)S(1)}, u32[]{:S(2)}, u32[]{:S(2)}) collective-permute-start(f32[2,512,1]{2,1,0:T(8,128)S(1)} %get-tuple-element.9), channel_id=1, source_target_pairs={{64,0},{128,64},{192,128},{256,192},{320,256},{384,320},{448,384},... | collective-permute-start | bytes 12296 | tf_op jit(solution)/shard_map/ppermute | solution.py:30
  109.4 3.9 %collective-permute-start.2 = (f32[2,512,1]{2,1,0:T(8,128)S(1)}, f32[2,512,1]{2,1,0:T(8,128)S(1)}, u32[]{:S(2)}, u32[]{:S(2)}) collective-permute-start(f32[2,512,1]{2,1,0:T(8,128)S(1)} %get-tuple-element.10), channel_id=1, source_target_pairs={{0,64},{64,128},{128,192},{192,256},{256,320},{320,384},{384,448},... | collective-permute-start | bytes 12296 | tf_op jit(solution)/shard_map/ppermute | solution.py:28
  113.4 9.4 %collective-permute-done.3 = f32[2,512,1]{2,1,0:T(8,128)S(1)} collective-permute-done((f32[2,512,1]{2,1,0:T(8,128)S(1)}, f32[2,512,1]{2,1,0:T(8,128)S(1)}, u32[]{:S(2)}, u32[]{:S(2)}) %collective-permute-start.3) | collective-permute-done | bytes 4128 | tf_op jit(solution)/shard_map/ppermute | solution.py:30
  122.8 5.5 %collective-permute-done.2 = f32[2,512,1]{2,1,0:T(8,128)S(1)} collective-permute-done((f32[2,512,1]{2,1,0:T(8,128)S(1)}, f32[2,512,1]{2,1,0:T(8,128)S(1)}, u32[]{:S(2)}, u32[]{:S(2)}) %collective-permute-start.2) | collective-permute-done | bytes 4128 | tf_op jit(solution)/shard_map/ppermute | solution.py:28
  128.8 0.8 fusion.4
  129.8 1.9 %collective-permute-start.5 = (f32[2,512,1]{2,1,0:T(8,128)S(1)}, f32[2,512,1]{2,1,0:T(8,128)S(1)}, u32[]{:S(2)}, u32[]{:S(2)}) collective-permute-start(f32[2,512,1]{2,1,0:T(8,128)S(1)} %get-tuple-element.7), channel_id=1, source_target_pairs={{64,0},{128,64},{192,128},{256,192},{320,256},{384,320},{448,384},... | collective-permute-start | bytes 12296 | tf_op jit(solution)/shard_map/ppermute | solution.py:30
  131.7 3.9 %collective-permute-start.4 = (f32[2,512,1]{2,1,0:T(8,128)S(1)}, f32[2,512,1]{2,1,0:T(8,128)S(1)}, u32[]{:S(2)}, u32[]{:S(2)}) collective-permute-start(f32[2,512,1]{2,1,0:T(8,128)S(1)} %get-tuple-element.8), channel_id=1, source_target_pairs={{0,64},{64,128},{128,192},{192,256},{256,320},{320,384},{384,448},... | collective-permute-start | bytes 12296 | tf_op jit(solution)/shard_map/ppermute | solution.py:28
  135.6 8.6 %collective-permute-done.5 = f32[2,512,1]{2,1,0:T(8,128)S(1)} collective-permute-done((f32[2,512,1]{2,1,0:T(8,128)S(1)}, f32[2,512,1]{2,1,0:T(8,128)S(1)}, u32[]{:S(2)}, u32[]{:S(2)}) %collective-permute-start.5) | collective-permute-done | bytes 4128 | tf_op jit(solution)/shard_map/ppermute | solution.py:30
  144.2 5.5 %collective-permute-done.4 = f32[2,512,1]{2,1,0:T(8,128)S(1)} collective-permute-done((f32[2,512,1]{2,1,0:T(8,128)S(1)}, f32[2,512,1]{2,1,0:T(8,128)S(1)}, u32[]{:S(2)}, u32[]{:S(2)}) %collective-permute-start.4) | collective-permute-done | bytes 4128 | tf_op jit(solution)/shard_map/ppermute | solution.py:28
  150.2 0.8 fusion.5
  151.2 1.9 %collective-permute-start.7 = (f32[2,512,1]{2,1,0:T(8,128)S(1)}, f32[2,512,1]{2,1,0:T(8,128)S(1)}, u32[]{:S(2)}, u32[]{:S(2)}) collective-permute-start(f32[2,512,1]{2,1,0:T(8,128)S(1)} %get-tuple-element.5), channel_id=1, source_target_pairs={{64,0},{128,64},{192,128},{256,192},{320,256},{384,320},{448,384},... | collective-permute-start | bytes 12296 | tf_op jit(solution)/shard_map/ppermute | solution.py:30
  153.1 3.9 %collective-permute-start.6 = (f32[2,512,1]{2,1,0:T(8,128)S(1)}, f32[2,512,1]{2,1,0:T(8,128)S(1)}, u32[]{:S(2)}, u32[]{:S(2)}) collective-permute-start(f32[2,512,1]{2,1,0:T(8,128)S(1)} %get-tuple-element.6), channel_id=1, source_target_pairs={{0,64},{64,128},{128,192},{192,256},{256,320},{320,384},{384,448},... | collective-permute-start | bytes 12296 | tf_op jit(solution)/shard_map/ppermute | solution.py:28
  157.1 7.7 %collective-permute-done.7 = f32[2,512,1]{2,1,0:T(8,128)S(1)} collective-permute-done((f32[2,512,1]{2,1,0:T(8,128)S(1)}, f32[2,512,1]{2,1,0:T(8,128)S(1)}, u32[]{:S(2)}, u32[]{:S(2)}) %collective-permute-start.7) | collective-permute-done | bytes 4128 | tf_op jit(solution)/shard_map/ppermute | solution.py:30
  164.8 5.5 %collective-permute-done.6 = f32[2,512,1]{2,1,0:T(8,128)S(1)} collective-permute-done((f32[2,512,1]{2,1,0:T(8,128)S(1)}, f32[2,512,1]{2,1,0:T(8,128)S(1)}, u32[]{:S(2)}, u32[]{:S(2)}) %collective-permute-start.6) | collective-permute-done | bytes 4128 | tf_op jit(solution)/shard_map/ppermute | solution.py:28
  170.8 1.5 fusion.6
  (33 shorter events, 11.3 us)
Async XLA Ops:
  0.0 88.2 %copy-start = (f32[512,1024]{1,0:T(8,128)S(1)}, f32[512,1024]{1,0:T(8,128)}, u32[]{:S(2)}) copy-start(f32[512,1024]{1,0:T(8,128)} %param.9) | copy-start | bytes 6291460
  8.0 12.0 %all-to-all-start = ((f32[8,1,2,1]{2,3,1,0:T(1,128)}), f32[8,1,2,1]{2,3,1,0:T(1,128)S(1)}, u32[]{:S(2)}, u32[]{:S(2)}) async-start(f32[8,1,2,1]{2,3,1,0:T(1,128)} %constant_dynamic-update-slice_fusion), calls=%async_computation | async-start | bytes 8192 | tf_op jit(solution)/shard_map/all_to_all | solution.py:16
  17.4 15.6 %copy-start.1 = (f32[128,128]{1,0:T(8,128)S(1)}, f32[128,128]{1,0:T(8,128)}, u32[]{:S(2)}) copy-start(f32[128,128]{1,0:T(8,128)} %param.7) | copy-start | bytes 196612
  20.0 12.1 %all-to-all-start.1 = ((f32[32,16,128]{2,0,1:T(8,128)}), f32[32,16,128]{2,0,1:T(8,128)S(1)}, u32[]{:S(2)}, u32[]{:S(2)}) async-start(f32[32,16,128]{2,0,1:T(8,128)} %copy.44), calls=%async_computation.1 | async-start | bytes 524288 | tf_op jit(solution)/shard_map/all_to_all | solution.py:58
  34.0 17.2 %copy-start.2 = (s32[2]{0:T(128)S(1)}, s32[2]{0:T(128)}, u32[]{:S(2)}) copy-start(s32[2]{0:T(128)} %param.8) | copy-start | bytes 28
  35.0 45.6 %all-to-all-start.2 = ((f32[128,8,128]{2,1,0:T(8,128)}), f32[128,8,128]{2,1,0:T(8,128)S(1)}, u32[]{:S(2)}, u32[]{:S(2)}) async-start(f32[128,8,128]{2,1,0:T(8,128)} %copy.48), calls=%async_computation.2 | async-start | bytes 1048576 | tf_op jit(solution)/shard_map/all_to_all | solution.py:68
  80.9 17.4 %collective-permute-start.1 = (f32[2,512,1]{2,1,0:T(8,128)S(1)}, f32[2,512,1]{2,1,0:T(8,128)S(1)}, u32[]{:S(2)}, u32[]{:S(2)}) collective-permute-start(f32[2,512,1]{2,1,0:T(8,128)S(1)} %get-tuple-element.11), channel_id=1, source_target_pairs={{64,0},{128,64},{192,128},{256,192},{320,256},{384,320},{448,384},... | collective-permute-start | bytes 12296 | tf_op jit(solution)/shard_map/ppermute | solution.py:30
  86.3 19.7 %collective-permute-start = (f32[2,512,1]{2,1,0:T(8,128)S(1)}, f32[2,512,1]{2,1,0:T(8,128)S(1)}, u32[]{:S(2)}, u32[]{:S(2)}) collective-permute-start(f32[2,512,1]{2,1,0:T(8,128)S(1)} %get-tuple-element.12), channel_id=1, source_target_pairs={{0,64},{64,128},{128,192},{192,256},{256,320},{320,384},{384,448},... | collective-permute-start | bytes 12296 | tf_op jit(solution)/shard_map/ppermute | solution.py:28
  107.5 15.3 %collective-permute-start.3 = (f32[2,512,1]{2,1,0:T(8,128)S(1)}, f32[2,512,1]{2,1,0:T(8,128)S(1)}, u32[]{:S(2)}, u32[]{:S(2)}) collective-permute-start(f32[2,512,1]{2,1,0:T(8,128)S(1)} %get-tuple-element.9), channel_id=1, source_target_pairs={{64,0},{128,64},{192,128},{256,192},{320,256},{384,320},{448,384},... | collective-permute-start | bytes 12296 | tf_op jit(solution)/shard_map/ppermute | solution.py:30
  109.4 18.9 %collective-permute-start.2 = (f32[2,512,1]{2,1,0:T(8,128)S(1)}, f32[2,512,1]{2,1,0:T(8,128)S(1)}, u32[]{:S(2)}, u32[]{:S(2)}) collective-permute-start(f32[2,512,1]{2,1,0:T(8,128)S(1)} %get-tuple-element.10), channel_id=1, source_target_pairs={{0,64},{64,128},{128,192},{192,256},{256,320},{320,384},{384,448},... | collective-permute-start | bytes 12296 | tf_op jit(solution)/shard_map/ppermute | solution.py:28
  129.8 14.4 %collective-permute-start.5 = (f32[2,512,1]{2,1,0:T(8,128)S(1)}, f32[2,512,1]{2,1,0:T(8,128)S(1)}, u32[]{:S(2)}, u32[]{:S(2)}) collective-permute-start(f32[2,512,1]{2,1,0:T(8,128)S(1)} %get-tuple-element.7), channel_id=1, source_target_pairs={{64,0},{128,64},{192,128},{256,192},{320,256},{384,320},{448,384},... | collective-permute-start | bytes 12296 | tf_op jit(solution)/shard_map/ppermute | solution.py:30
  131.7 18.0 %collective-permute-start.4 = (f32[2,512,1]{2,1,0:T(8,128)S(1)}, f32[2,512,1]{2,1,0:T(8,128)S(1)}, u32[]{:S(2)}, u32[]{:S(2)}) collective-permute-start(f32[2,512,1]{2,1,0:T(8,128)S(1)} %get-tuple-element.8), channel_id=1, source_target_pairs={{0,64},{64,128},{128,192},{192,256},{256,320},{320,384},{384,448},... | collective-permute-start | bytes 12296 | tf_op jit(solution)/shard_map/ppermute | solution.py:28
  151.2 13.6 %collective-permute-start.7 = (f32[2,512,1]{2,1,0:T(8,128)S(1)}, f32[2,512,1]{2,1,0:T(8,128)S(1)}, u32[]{:S(2)}, u32[]{:S(2)}) collective-permute-start(f32[2,512,1]{2,1,0:T(8,128)S(1)} %get-tuple-element.5), channel_id=1, source_target_pairs={{64,0},{128,64},{192,128},{256,192},{320,256},{384,320},{448,384},... | collective-permute-start | bytes 12296 | tf_op jit(solution)/shard_map/ppermute | solution.py:30
  153.1 17.2 %collective-permute-start.6 = (f32[2,512,1]{2,1,0:T(8,128)S(1)}, f32[2,512,1]{2,1,0:T(8,128)S(1)}, u32[]{:S(2)}, u32[]{:S(2)}) collective-permute-start(f32[2,512,1]{2,1,0:T(8,128)S(1)} %get-tuple-element.6), channel_id=1, source_target_pairs={{0,64},{64,128},{128,192},{192,256},{256,320},{320,384},{384,448},... | collective-permute-start | bytes 12296 | tf_op jit(solution)/shard_map/ppermute | solution.py:28
